TPU v7x, 32 devices: a whole 2x2x4 slice. The times are simulated.
32 devices in a mesh: region: 16 (over z, x, core), event: 2 (over y).
Axes of the slice: x: 2, y: 2, z: 4, core: 2. Of those that a mesh axis runs over, the one named last changes fastest.
Arguments:
- forward_field: float32 [2, 3, 128, 9, 128], P('event', None, 'region'), may hold values from -6 to 6
- forward_speed: float32 [2, 3, 128, 9, 128], P('event', None, 'region'), may hold values from -6 to 6
- adjoint_field: float32 [2, 3, 128, 9, 128], P('event', None, 'region'), may hold values from -6 to 6
- adjoint_speed: float32 [2, 3, 128, 9, 128], P('event', None, 'region'), may hold values from -6 to 6
- adjoint_source: float32 [2, 3, 128, 9, 128], P('event', None, 'region'), may hold values from -6 to 6
- lame_lambda: float32 [128, 9, 128], P('region'), may hold values from 0.5 to 2
- lame_mu: float32 [128, 9, 128], P('region'), may hold values from 0.3 to 1.2
- density: float32 [128, 9, 128], P('region'), may hold values from 0.8 to 2.4
Outputs:
- forward_out: float32 [2, 3, 128, 9, 128], P('event', None, 'region')
- forward_speed_out: float32 [2, 3, 128, 9, 128], P('event', None, 'region')
- adjoint_out: float32 [2, 3, 128, 9, 128], P('event', None, 'region')
- adjoint_speed_out: float32 [2, 3, 128, 9, 128], P('event', None, 'region')
- kernels: float32 [2, 128, 9, 128], P(None, ('region', 'event'))
All inputs are finite; a program needn't handle non-finite values.
Results may differ from a plain program's by a relative error of at most 0.0003.
Values sent between devices are 32-bit elements; how exact they have to be, the bound alone decides.
A program may use at most 64 MiB of HBM per device.

v0:
```python
import functools
import math

import jax
import jax.numpy as jnp
import numpy as np
from jax import lax
from jax.experimental import pallas as pl
from jax.experimental.pallas import tpu as pltpu
from jax.sharding import PartitionSpec as P

STEPS = 2
time_step = 0.02
MESH = pl.DeviceIdType.MESH


def gll_numbers():
    points = np.array([-1.0, -math.sqrt(3.0 / 7.0), 0.0, math.sqrt(3.0 / 7.0), 1.0])
    weights = np.array([0.1, 49.0 / 90.0, 32.0 / 45.0, 49.0 / 90.0, 0.1])
    legendre = (35.0 * points**4 - 30.0 * points**2 + 3.0) / 8.0
    derivative = np.zeros((5, 5))
    for target in range(5):
        for column in range(5):
            if target != column:
                derivative[target, column] = legendre[target] / (
                    legendre[column] * (points[target] - points[column])
                )
    derivative[0, 0] = -5.0
    derivative[4, 4] = 5.0
    return (derivative, weights)


def lane_tables(lanes):
    numbers, _ = gll_numbers()
    table = np.zeros((lanes, 2 * lanes))
    for lane in range(lanes):
        start, local = lane - lane % 4, lane % 4
        for source in range(5):
            if local:
                table[(start + source) % lanes, lane] += numbers[local, source]
            else:
                right, left = (start + source) % lanes, (start - 4 + source) % lanes
                table[right, lane] += 0.5 * numbers[0, source]
                table[left, lane] += 0.5 * numbers[4, source]
                table[right, lanes + lane] += 0.5 * numbers[0, source]
                table[left, lanes + lane] -= 0.5 * numbers[4, source]
    high = table.astype(np.float32).astype(jnp.bfloat16)
    low = (table - high.astype(np.float64)).astype(np.float32).astype(jnp.bfloat16)
    return (
        np.concatenate([high, high], axis=0),
        low,
        np.concatenate([high.T, low.T], axis=1),
        np.ascontiguousarray(high.T),
    )


def combine(coefficients, pieces):
    total = None
    for number, piece in zip(coefficients, pieces):
        if number != 0.0:
            term = float(number) * piece
            total = term if total is None else total + term
    return total


def turn(value, shift):
    return pltpu.roll(value, shift % 8, value.ndim - 2)


def row_bit(shape, bit):
    return (lax.broadcasted_iota(jnp.int32, shape, len(shape) - 2) & bit) == 0


def swap_rows(four):
    shape = four[0].shape
    low_two, low_one = row_bit(shape, 2), row_bit(shape, 1)
    a0, a1, a2, a3 = four
    b0 = jnp.where(low_two, a0, turn(a2, 2))
    b2 = jnp.where(low_two, turn(a0, -2), a2)
    b1 = jnp.where(low_two, a1, turn(a3, 2))
    b3 = jnp.where(low_two, turn(a1, -2), a3)
    return (
        jnp.where(low_one, b0, turn(b1, 1)),
        jnp.where(low_one, turn(b0, -1), b1),
        jnp.where(low_one, b2, turn(b3, 1)),
        jnp.where(low_one, turn(b2, -1), b3),
    )


def middle_sum(blocks):
    first, last = blocks[..., 0, :, :], blocks[..., 4, :, :]
    low = row_bit(first.shape, 1)
    new_last = last + jnp.where(low, turn(first, -1), 0.0)
    new_first = first + jnp.where(low, 0.0, turn(last, 1))
    return jnp.concatenate(
        [new_first[..., None, :, :], blocks[..., 1:4, :, :], new_last[..., None, :, :]], axis=-3
    )


def pack_half(blocks, low):
    half = (blocks.shape[0] + 1) // 2
    first, second = blocks[:half], blocks[half:]
    if second.shape[0] < half:
        second = jnp.concatenate([second, first[-1:]], axis=0)
    keep = row_bit(first.shape, 4)
    other = turn(second, 4)
    return jnp.where(keep, first, other) if low else jnp.where(keep, other, first)


def unpack_half(packed, count):
    return jnp.concatenate([packed, turn(packed, 4)], axis=0)[:count]


def kernel(
    regions,
    events,
    uf,
    vf,
    ua,
    va,
    source,
    lam,
    mu,
    rho,
    slope_two,
    slope_low,
    back_two,
    back_high,
    uf_out,
    vf_out,
    ua_out,
    va_out,
    k_out,
    u,
    b,
    sm,
    im,
    muw,
    lamw,
    gy,
    sx,
    sy,
    f,
    w8,
    kacc,
    send_a,
    recv_a,
    send_b,
    recv_b,
    send_l,
    recv_l,
    send_r,
    recv_r,
    send_8,
    recv_8,
    send_k,
    recv_k,
    sems,
    sems_8,
    sems_k,
):
    numbers, weights = gll_numbers()
    lanes = u.shape[-1]
    region, event = lax.axis_index("region"), lax.axis_index("event")
    left, right = lax.rem(region + regions - 1, regions), lax.rem(region + 1, regions)
    planes = 8 // events

    barrier = pltpu.get_barrier_semaphore()
    for other in range(events):
        for side in (left, right):
            pl.semaphore_signal(barrier, inc=1, device_id=(side, other), device_id_type=MESH)
    for offset in range(1, events):
        partner = lax.rem(event + offset, events)
        pl.semaphore_signal(barrier, inc=1, device_id=(region, partner), device_id_type=MESH)

    def remote(src, dst, number, target):
        return pltpu.make_async_remote_copy(
            src_ref=src,
            dst_ref=dst,
            send_sem=sems.at[0, number],
            recv_sem=sems.at[1, number],
            device_id=target,
            device_id_type=MESH,
        )

    one = (5, 8, lanes)
    low4, low2, low1 = row_bit(one, 4), row_bit(one, 2), row_bit(one, 1)
    lane_place = lax.broadcasted_iota(jnp.int32, one, 2) & 3
    lane_weight = jnp.where(
        lane_place == 0, 0.2, jnp.where(lane_place == 2, 32.0 / 45.0, 49.0 / 90.0)
    ).astype(jnp.float32)
    level = lax.broadcasted_iota(jnp.int32, one, 0)
    edge = (level == 0) | (level == 4)
    inner = jnp.where(level == 2, 32.0 / 45.0, 49.0 / 90.0)
    level_weight = jnp.where(edge, 0.1, inner).astype(jnp.float32)
    closed = ((level == 0) & low1) | ((level == 4) & jnp.logical_not(low1))
    node_weight = jnp.where(edge, jnp.where(closed, 0.1, 0.2), inner).astype(jnp.float32)

    def take(first, second):
        return swap_rows((first[0:5], first[4:9], second[0:5], second[4:9]))

    for comp in range(3):
        for place, value in enumerate(take(uf[comp], ua[comp])):
            u[place, comp] = value
    lam_here, mu_here = take(lam[...], lam[...]), take(mu[...], mu[...])
    edge_pair = jnp.where(low2, mu_here[0], lam_here[0])
    send_a[...] = pack_half(
        jnp.concatenate([u[0].reshape(15, 8, lanes), edge_pair], axis=0), True
    )
    pl.semaphore_wait(barrier, 2 * events + events - 1)
    copy_a = remote(send_a, recv_a, 0, (left, event))
    copy_a.start()

    rho_here = take(rho[...], rho[...])
    for place in range(4):
        weight = 0.2 if place == 0 else float(weights[place])
        im[place] = time_step / (rho_here[place] * (weight * (node_weight * lane_weight)))
    for comp in range(3):
        rates = take(vf[comp], va[comp])
        sources = take(jnp.zeros_like(source[comp]), source[comp])
        for place in range(4):
            pushed = sources[place] * im[place]
            sm[place, comp] = pushed
            b[place, comp] = rates[place] + pushed
    ahead = u[0] + time_step * b[0]
    send_b[...] = pack_half(
        jnp.concatenate([ahead.reshape(15, 8, lanes), time_step * im[0]], axis=0), True
    )
    copy_b = remote(send_b, recv_b, 1, (left, event))
    copy_b.start()

    for place in range(4):
        weight = float(weights[place]) * (level_weight * lane_weight)
        muw[place] = mu_here[place] * weight
        lamw[place] = lam_here[place] * weight

    def slopes(begin, end):
        rows = (end - begin) * 120
        values = u[begin:end].reshape(rows, lanes)
        high = values.astype(jnp.bfloat16)
        low = (values - high.astype(jnp.float32)).astype(jnp.bfloat16)
        found = jnp.dot(
            jnp.concatenate([high, low], axis=1), slope_two[...], preferred_element_type=jnp.float32
        ) + jnp.dot(high, slope_low[...], preferred_element_type=jnp.float32)
        gy[begin:end] = found.reshape(end - begin, 3, 5, 8, 2 * lanes)

    def strains(step):
        for i in range(5):
            gx = [combine(numbers[i], [u[q, c] for q in range(5)]) for c in range(3)]
            gz = []
            for c in range(3):
                levels = [u[i, c, q] for q in range(5)]
                gz.append(jnp.stack([combine(numbers[k], levels) for k in range(5)]))
            gm = [gy[i, c, :, :, :lanes] for c in range(3)]
            gd = [gy[i, c, :, :, lanes:] for c in range(3)]
            m, l = muw[i], lamw[i]
            xz, xy, zy = gx[1] + gz[0], gx[2] + gm[0], gz[2] + gm[1]
            dilation = gx[0] + gz[1] + gm[2]
            both = m + m
            press = l * dilation
            s_xz, s_xy, s_zy = m * xz, m * xy, m * zy
            sx[i, 0] = both * gx[0] + press
            sx[i, 1] = s_xz
            sx[i, 2] = s_xy
            sy[i, 0, :, :, :lanes] = s_xy
            sy[i, 1, :, :, :lanes] = s_zy
            sy[i, 2, :, :, :lanes] = both * gm[2] + press
            sy[i, 0, :, :, lanes:] = m * gd[0]
            sy[i, 1, :, :, lanes:] = m * gd[1]
            sy[i, 2, :, :, lanes:] = (both + l) * gd[2]
            for c, stress in enumerate((s_xz, both * gz[1] + press, s_zy)):
                levels = [stress[q] for q in range(5)]
                f[i, c] = jnp.stack([combine(numbers[:, k], levels) for k in range(5)])

            def product(value):
                return value * turn(value, -2)

            jump = product(gd[2])
            weight = float(weights[i]) * (level_weight * lane_weight)
            k1 = weight * (product(dilation) + jump)
            shear = product(gx[0]) + product(gz[1]) + product(gm[2]) + jump
            cross = product(xz) + product(xy) + product(zy) + product(gd[0]) + product(gd[1])
            k2 = weight * (2.0 * shear + cross)
            both_kinds = jnp.where(low2, k1, turn(k2, 2))
            kacc[i] = both_kinds if step == 0 else kacc[i] + both_kinds

    def gather_forces():
        rows = 600
        values = sy[...].reshape(rows, 2 * lanes)
        high = values.astype(jnp.bfloat16)
        low = (values - high.astype(jnp.float32)).astype(jnp.bfloat16)
        first = jnp.dot(high, back_two[...], preferred_element_type=jnp.float32)
        total = first[:, :lanes] + first[:, lanes:]
        total = total + jnp.dot(low, back_high[...], preferred_element_type=jnp.float32)
        total = total.reshape(5, 3, 5, 8, lanes)
        for i in (0, 4, 1, 2, 3):
            for c in range(3):
                value = f[i, c] + total[i, c] + combine(numbers[:, i], [sx[p, c] for p in range(5)])
                f[i, c] = middle_sum(value)

    slopes(0, 4)
    copy_a.wait_recv()
    arrived = unpack_half(recv_a[...], 20)
    wide = jnp.broadcast_to(row_bit((8, lanes), 4), (15, 8, lanes))
    next_plane = turn(jnp.where(wide, arrived[:15], u[0].reshape(15, 8, lanes)), 4)
    u[4] = next_plane.reshape(3, 5, 8, lanes)
    pair = arrived[15:]
    mu_next, lam_next = jnp.where(low2, pair, turn(pair, 2)), jnp.where(low2, turn(pair, -2), pair)
    weight = 0.1 * (level_weight * lane_weight)
    muw[4] = turn(jnp.where(low4, mu_next, mu_here[0]), 4) * weight
    lamw[4] = turn(jnp.where(low4, lam_next, lam_here[0]), 4) * weight
    slopes(4, 5)
    strains(0)
    gather_forces()
    send_l[...] = pack_half(f[0].reshape(15, 8, lanes), True)
    send_r[0] = pack_half(f[4].reshape(15, 8, lanes), False)
    copy_l = remote(send_l, recv_l, 2, (left, event))
    copy_l.start()
    copy_r = remote(send_r.at[0], recv_r.at[0], 3, (right, event))
    copy_r.start()

    def advance(place, force):
        for c in range(3):
            rate = b[place, c] - im[place] * force[c]
            b[place, c] = rate
            u[place, c] = u[place, c] + time_step * rate

    for place in (1, 2, 3):
        advance(place, f[place])
        b[place] = b[place] + sm[place]
    slopes(1, 4)
    copy_b.wait_recv()
    later = unpack_half(recv_b[...], 20)
    copy_l.wait_recv()
    from_right = unpack_half(recv_l[...], 15)
    own_last = f[4].reshape(15, 8, lanes)
    full = own_last + turn(from_right, 4)
    heavy = jnp.broadcast_to(later[15:][None], (3, 5, 8, lanes)).reshape(15, 8, lanes)
    u8 = turn(later[:15], 4) - turn(heavy, 4) * full

    def first_force(slot):
        from_left = unpack_half(recv_r[slot], 15)
        mixed = turn(jnp.where(wide, own_last_of(), from_left), 4)
        return (f[0].reshape(15, 8, lanes) + mixed).reshape(3, 5, 8, lanes)

    def own_last_of():
        return f[4].reshape(15, 8, lanes)

    copy_r.wait_recv()
    advance(0, first_force(0))
    b[0] = b[0] + sm[0]
    shared = turn(u[0].reshape(15, 8, lanes), 4)
    u[4] = jnp.where(wide, shared, u8).reshape(3, 5, 8, lanes)
    slopes(0, 1)
    slopes(4, 5)
    strains(1)
    gather_forces()
    send_r[1] = pack_half(f[4].reshape(15, 8, lanes), False)
    copy_s = remote(send_r.at[1], recv_r.at[1], 4, (right, event))
    copy_s.start()

    for i in range(5):
        kacc[i] = middle_sum(kacc[i])
    send_8[...] = kacc[4]
    copy_8 = pltpu.make_async_remote_copy(
        src_ref=send_8,
        dst_ref=recv_8.at[event],
        send_sem=sems.at[0, 5],
        recv_sem=sems_8.at[event],
        device_id=(right, 0),
        device_id_type=MESH,
    )
    copy_8.start()
    first_plane = kacc[0] + jnp.where(low4, 0.0, turn(kacc[4], 4))
    nodes = swap_rows((first_plane, kacc[1], kacc[2], kacc[3]))
    for kind in range(2):
        whole = jnp.concatenate([nodes[2 * kind][0:4], nodes[2 * kind + 1]], axis=0)
        for owner in range(events):
            send_k[owner, kind] = whole[:, planes * owner : planes * owner + planes]
    copies = []
    for offset in range(1, events):
        partner = lax.rem(event + offset, events)
        copy = pltpu.make_async_remote_copy(
            src_ref=send_k.at[partner],
            dst_ref=recv_k.at[offset - 1],
            send_sem=sems_k.at[0, offset - 1],
            recv_sem=sems_k.at[1, offset - 1],
            device_id=(region, partner),
            device_id_type=MESH,
        )
        copy.start()
        copies.append(copy)

    for place in (1, 2, 3):
        advance(place, f[place])
    copy_s.wait_recv()
    advance(0, first_force(1))

    def give(state, forward_out, adjoint_out):
        for c in range(3):
            four = swap_rows((state[0, c], state[1, c], state[2, c], state[3, c]))
            forward_out[c] = jnp.concatenate([four[0][0:4], four[1]], axis=0)
            adjoint_out[c] = jnp.concatenate([four[2][0:4], four[3]], axis=0)

    give(u, uf_out, ua_out)
    give(b, vf_out, va_out)

    total = send_k[event]
    for offset in range(1, events):
        copies[offset - 1].wait_recv()
        total = total + recv_k[offset - 1]
    k_out[...] = total

    @pl.when(event == 0)
    def _():
        extra = None
        for other in range(events):
            pltpu.make_async_copy(recv_8.at[other], recv_8.at[other], sems_8.at[other]).wait()
            extra = recv_8[other] if extra is None else extra + recv_8[other]
        extra = jnp.where(low4, turn(extra, 4), 0.0)
        nothing = jnp.zeros_like(extra)
        parts = swap_rows((extra, nothing, nothing, nothing))
        for kind in range(2):
            whole = jnp.concatenate([parts[2 * kind][0:4], parts[2 * kind + 1]], axis=0)
            k_out[kind] = k_out[kind] + whole[:, 0:planes]

    for copy in [copy_a, copy_b, copy_l, copy_r, copy_s, copy_8] + copies:
        copy.wait_send()


def run(regions, events, interpret, *arrays):
    lanes = arrays[0].shape[-1]
    fields = [jnp.transpose(array[0], (0, 2, 1, 3)) for array in arrays[:5]]
    models = [jnp.transpose(array, (1, 0, 2)) for array in arrays[5:]]
    tables = [jnp.asarray(table) for table in lane_tables(lanes)]
    planes = 8 // events
    state = jax.ShapeDtypeStruct((3, 9, 8, lanes), jnp.float32)
    f32 = jnp.float32
    vector = pltpu.VMEM((5, 3, 5, 8, lanes), f32)
    wide = pltpu.VMEM((5, 3, 5, 8, 2 * lanes), f32)
    scalar = pltpu.VMEM((5, 5, 8, lanes), f32)

    def packed(*lead):
        return pltpu.VMEM(lead + (8, lanes), f32)

    outs = pl.pallas_call(
        functools.partial(kernel, regions, events),
        out_shape=[state] * 4 + [jax.ShapeDtypeStruct((2, 9, planes, lanes), f32)],
        in_specs=[pl.BlockSpec(memory_space=pltpu.VMEM)] * 12,
        out_specs=[pl.BlockSpec(memory_space=pltpu.VMEM)] * 5,
        scratch_shapes=[
            vector,
            vector,
            vector,
            scalar,
            scalar,
            scalar,
            wide,
            vector,
            wide,
            vector,
            packed(15),
            scalar,
            packed(10),
            packed(10),
            packed(10),
            packed(10),
            packed(8),
            packed(8),
            packed(2, 8),
            packed(2, 8),
            packed(5),
            packed(events, 5),
            pltpu.VMEM((events, 2, 9, planes, lanes), f32),
            pltpu.VMEM((max(events - 1, 1), 2, 9, planes, lanes), f32),
            pltpu.SemaphoreType.DMA((2, 6)),
            pltpu.SemaphoreType.DMA((events,)),
            pltpu.SemaphoreType.DMA((2, max(events - 1, 1))),
        ],
        compiler_params=pltpu.CompilerParams(
            collective_id=0, has_side_effects=True, vmem_limit_bytes=40 * 1024 * 1024
        ),
        name="adjoint_steps",
    )(*fields, *models, *tables)
    forward, forward_rate, adjoint, adjoint_rate = [
        jnp.transpose(out, (0, 2, 1, 3))[None] for out in outs[:4]
    ]
    return (forward, forward_rate, adjoint, adjoint_rate, jnp.transpose(outs[4], (0, 2, 1, 3)))


def solution(mesh):
    field = P("event", None, "region", None, None)
    model = P("region", None, None)
    regions, events = mesh.shape["region"], mesh.shape["event"]
    return jax.shard_map(
        functools.partial(run, regions, events, False),
        mesh=mesh,
        in_specs=(field,) * 5 + (model,) * 3,
        out_specs=(field,) * 4 + (P(None, ("region", "event"), None, None),),
        check_vma=False,
    )
```

profile of v0, /device:TPU:0, one launch (start us, length us, event | category | flops | bytes accessed | tf_op | source)
XLA Modules:
  0.0 32.7 jit_solution(18342198801355469812)
XLA Ops:
  0.6 0.0 copy-start
  0.6 0.9 %copy-done = bf16[256,256]{1,0:T(8,128)(2,1)S(1)} copy-done((bf16[256,256]{1,0:T(8,128)(2,1)S(1)}, bf16[256,256]{1,0:T(8,128)(2,1)}, u32[]{:S(2)}) %copy-start) | copy-done | bytes 131096
  1.5 0.0 copy-start.1
  1.5 0.9 %copy-done.1 = bf16[256,256]{1,0:T(8,128)(2,1)S(1)} copy-done((bf16[256,256]{1,0:T(8,128)(2,1)S(1)}, bf16[256,256]{1,0:T(8,128)(2,1)}, u32[]{:S(2)}) %copy-start.1) | copy-done | bytes 131096
  2.4 0.0 copy-start.2
  2.4 0.9 %copy-done.2 = f32[1,3,8,9,128]{4,2,3,1,0:T(8,128)S(1)} copy-done((f32[1,3,8,9,128]{4,2,3,1,0:T(8,128)S(1)}, f32[1,3,8,9,128]{4,2,3,1,0:T(8,128)}, u32[]{:S(2)}) %copy-start.2) | copy-done | bytes 110616
  3.3 0.0 copy-start.3
  3.3 0.9 %copy-done.3 = f32[1,3,8,9,128]{4,2,3,1,0:T(8,128)S(1)} copy-done((f32[1,3,8,9,128]{4,2,3,1,0:T(8,128)S(1)}, f32[1,3,8,9,128]{4,2,3,1,0:T(8,128)}, u32[]{:S(2)}) %copy-start.3) | copy-done | bytes 110616
  4.2 0.0 copy-start.4
  4.2 0.9 %copy-done.4 = f32[1,3,8,9,128]{4,2,3,1,0:T(8,128)S(1)} copy-done((f32[1,3,8,9,128]{4,2,3,1,0:T(8,128)S(1)}, f32[1,3,8,9,128]{4,2,3,1,0:T(8,128)}, u32[]{:S(2)}) %copy-start.4) | copy-done | bytes 110616
  5.1 0.0 copy-start.5
  5.1 0.9 %copy-done.5 = f32[1,3,8,9,128]{4,2,3,1,0:T(8,128)S(1)} copy-done((f32[1,3,8,9,128]{4,2,3,1,0:T(8,128)S(1)}, f32[1,3,8,9,128]{4,2,3,1,0:T(8,128)}, u32[]{:S(2)}) %copy-start.5) | copy-done | bytes 110616
  6.0 0.0 copy-start.6
  6.0 0.9 %copy-done.6 = f32[1,3,8,9,128]{4,2,3,1,0:T(8,128)S(1)} copy-done((f32[1,3,8,9,128]{4,2,3,1,0:T(8,128)S(1)}, f32[1,3,8,9,128]{4,2,3,1,0:T(8,128)}, u32[]{:S(2)}) %copy-start.6) | copy-done | bytes 110616
  6.9 0.0 copy-start.7
  6.9 0.8 %copy-done.7 = bf16[256,128]{1,0:T(8,128)(2,1)S(1)} copy-done((bf16[256,128]{1,0:T(8,128)(2,1)S(1)}, bf16[256,128]{1,0:T(8,128)(2,1)}, u32[]{:S(2)}) %copy-start.7) | copy-done | bytes 65560
  7.8 0.0 copy-start.8
  7.8 0.8 %copy-done.8 = bf16[128,256]{1,0:T(8,128)(2,1)S(1)} copy-done((bf16[128,256]{1,0:T(8,128)(2,1)S(1)}, bf16[128,256]{1,0:T(8,128)(2,1)}, u32[]{:S(2)}) %copy-start.8) | copy-done | bytes 65560
  8.6 0.0 copy-start.9
  8.6 0.8 %copy-done.9 = f32[8,9,128]{2,0,1:T(8,128)S(1)} copy-done((f32[8,9,128]{2,0,1:T(8,128)S(1)}, f32[8,9,128]{2,0,1:T(8,128)}, u32[]{:S(2)}) %copy-start.9) | copy-done | bytes 36888
  9.4 0.0 copy-start.10
  9.4 0.8 %copy-done.10 = f32[8,9,128]{2,0,1:T(8,128)S(1)} copy-done((f32[8,9,128]{2,0,1:T(8,128)S(1)}, f32[8,9,128]{2,0,1:T(8,128)}, u32[]{:S(2)}) %copy-start.10) | copy-done | bytes 36888
  10.2 0.0 copy-start.11
  10.2 0.8 %copy-done.11 = f32[8,9,128]{2,0,1:T(8,128)S(1)} copy-done((f32[8,9,128]{2,0,1:T(8,128)S(1)}, f32[8,9,128]{2,0,1:T(8,128)}, u32[]{:S(2)}) %copy-start.11) | copy-done | bytes 36888
  10.9 18.5 %adjoint_steps.1 = (f32[3,9,8,128]{3,2,1,0:T(8,128)S(1)}, f32[3,9,8,128]{3,2,1,0:T(8,128)S(1)}, f32[3,9,8,128]{3,2,1,0:T(8,128)S(1)}, f32[3,9,8,128]{3,2,1,0:T(8,128)S(1)}, f32[2,9,4,128]{3,2,1,0:T(4,128)S(1)}) custom-call(f32[3,9,8,128]{3,2,1,0:T(8,128)S(1)} %bitcast.31, f32[3,9,8,128]{3,2,1,0:T(8,128)S(1)} %bitcast.32, f32[3,9,8,128]{3,2,1,0:T(8,128)S(1)} %bitcast.33, ...), custom_call_target="tpu_custom_call" | custom-call | tf_op jit(solution)/shard_map/adjoint_steps/pallas_call | solution.py:446
  29.5 0.6 %copy.22 = f32[1,3,8,9,128]{4,2,3,1,0:T(8,128)} copy(f32[1,3,8,9,128]{4,2,3,1,0:T(8,128)S(1)} %bitcast.39) | data formatting | bytes 221184
  30.1 0.6 %copy.23 = f32[1,3,8,9,128]{4,2,3,1,0:T(8,128)} copy(f32[1,3,8,9,128]{4,2,3,1,0:T(8,128)S(1)} %bitcast.38) | data formatting | bytes 221184
  30.8 0.6 %copy.24 = f32[1,3,8,9,128]{4,2,3,1,0:T(8,128)} copy(f32[1,3,8,9,128]{4,2,3,1,0:T(8,128)S(1)} %bitcast.37) | data formatting | bytes 221184
  31.4 0.6 %copy.25 = f32[1,3,8,9,128]{4,2,3,1,0:T(8,128)} copy(f32[1,3,8,9,128]{4,2,3,1,0:T(8,128)S(1)} %bitcast.36) | data formatting | bytes 221184
  32.1 0.6 %copy.26 = f32[2,4,9,128]{3,1,2,0:T(4,128)} copy(f32[2,4,9,128]{3,1,2,0:T(4,128)S(1)} %bitcast.43) | data formatting | bytes 73728
Async XLA Ops:
  0.6 0.9 %copy-start = (bf16[256,256]{1,0:T(8,128)(2,1)S(1)}, bf16[256,256]{1,0:T(8,128)(2,1)}, u32[]{:S(2)}) copy-start(bf16[256,256]{1,0:T(8,128)(2,1)} %constant.10.clone.back_two) | copy-start | bytes 393220
  1.5 0.9 %copy-start.1 = (bf16[256,256]{1,0:T(8,128)(2,1)S(1)}, bf16[256,256]{1,0:T(8,128)(2,1)}, u32[]{:S(2)}) copy-start(bf16[256,256]{1,0:T(8,128)(2,1)} %constant.8.clone.slope_two) | copy-start | bytes 393220
  2.4 0.9 %copy-start.2 = (f32[1,3,8,9,128]{4,2,3,1,0:T(8,128)S(1)}, f32[1,3,8,9,128]{4,2,3,1,0:T(8,128)}, u32[]{:S(2)}) copy-start(f32[1,3,8,9,128]{4,2,3,1,0:T(8,128)} %param.12) | copy-start | bytes 331780
  3.3 0.9 %copy-start.3 = (f32[1,3,8,9,128]{4,2,3,1,0:T(8,128)S(1)}, f32[1,3,8,9,128]{4,2,3,1,0:T(8,128)}, u32[]{:S(2)}) copy-start(f32[1,3,8,9,128]{4,2,3,1,0:T(8,128)} %param.13) | copy-start | bytes 331780
  4.2 0.9 %copy-start.4 = (f32[1,3,8,9,128]{4,2,3,1,0:T(8,128)S(1)}, f32[1,3,8,9,128]{4,2,3,1,0:T(8,128)}, u32[]{:S(2)}) copy-start(f32[1,3,8,9,128]{4,2,3,1,0:T(8,128)} %param.14) | copy-start | bytes 331780
  5.1 0.9 %copy-start.5 = (f32[1,3,8,9,128]{4,2,3,1,0:T(8,128)S(1)}, f32[1,3,8,9,128]{4,2,3,1,0:T(8,128)}, u32[]{:S(2)}) copy-start(f32[1,3,8,9,128]{4,2,3,1,0:T(8,128)} %param.15) | copy-start | bytes 331780
  6.0 0.9 %copy-start.6 = (f32[1,3,8,9,128]{4,2,3,1,0:T(8,128)S(1)}, f32[1,3,8,9,128]{4,2,3,1,0:T(8,128)}, u32[]{:S(2)}) copy-start(f32[1,3,8,9,128]{4,2,3,1,0:T(8,128)} %param.16) | copy-start | bytes 331780
  6.9 0.8 %copy-start.7 = (bf16[256,128]{1,0:T(8,128)(2,1)S(1)}, bf16[256,128]{1,0:T(8,128)(2,1)}, u32[]{:S(2)}) copy-start(bf16[256,128]{1,0:T(8,128)(2,1)} %constant.11.clone.back_high) | copy-start | bytes 196612
  7.8 0.8 %copy-start.8 = (bf16[128,256]{1,0:T(8,128)(2,1)S(1)}, bf16[128,256]{1,0:T(8,128)(2,1)}, u32[]{:S(2)}) copy-start(bf16[128,256]{1,0:T(8,128)(2,1)} %constant.9.clone.slope_low) | copy-start | bytes 196612
  8.6 0.8 %copy-start.9 = (f32[8,9,128]{2,0,1:T(8,128)S(1)}, f32[8,9,128]{2,0,1:T(8,128)}, u32[]{:S(2)}) copy-start(f32[8,9,128]{2,0,1:T(8,128)} %param.17) | copy-start | bytes 110596
  9.4 0.8 %copy-start.10 = (f32[8,9,128]{2,0,1:T(8,128)S(1)}, f32[8,9,128]{2,0,1:T(8,128)}, u32[]{:S(2)}) copy-start(f32[8,9,128]{2,0,1:T(8,128)} %param.18) | copy-start | bytes 110596
  10.2 0.8 %copy-start.11 = (f32[8,9,128]{2,0,1:T(8,128)S(1)}, f32[8,9,128]{2,0,1:T(8,128)}, u32[]{:S(2)}) copy-start(f32[8,9,128]{2,0,1:T(8,128)} %param.19) | copy-start | bytes 110596
where the time goes:
time: 33.2 us; the launch traced here: 32.7 us
  Pallas kernels  18.5 us (56%)
  local copies, waits for them, and re-layouts  13.5 us (41%)
  between operations  0.66 us (2%)
    pallas_call x1, Pallas kernels, run(): pl.pallas_call(functools.partial(kernel, regions, events), out_shape=[sta...  18.5 us
    unnamed x29, local copies, waits for them, and re-layouts  13.5 us

commit v1 on v0

--- a/solution.py
+++ b/solution.py
@@ -114,18 +114,18 @@
 def kernel(
     regions,
     events,
-    uf,
-    vf,
-    ua,
-    va,
-    source,
-    lam,
-    mu,
-    rho,
-    slope_two,
-    slope_low,
-    back_two,
-    back_high,
+    uf_in,
+    vf_in,
+    ua_in,
+    va_in,
+    source_in,
+    lam_in,
+    mu_in,
+    rho_in,
+    slope_two_in,
+    slope_low_in,
+    back_two_in,
+    back_high_in,
     uf_out,
     vf_out,
     ua_out,
@@ -158,6 +158,19 @@
     sems,
     sems_8,
     sems_k,
+    uf,
+    vf,
+    ua,
+    va,
+    source,
+    lam,
+    mu,
+    rho,
+    slope_two,
+    slope_low,
+    back_two,
+    back_high,
+    load_sems,
 ):
     numbers, weights = gll_numbers()
     lanes = u.shape[-1]
@@ -172,6 +185,30 @@
     for offset in range(1, events):
         partner = lax.rem(event + offset, events)
         pl.semaphore_signal(barrier, inc=1, device_id=(region, partner), device_id_type=MESH)
+
+    loads = {}
+    for number, (name, src, dst) in enumerate(
+        (
+            ("uf", uf_in, uf),
+            ("ua", ua_in, ua),
+            ("lam", lam_in, lam),
+            ("mu", mu_in, mu),
+            ("rho", rho_in, rho),
+            ("vf", vf_in, vf),
+            ("va", va_in, va),
+            ("source", source_in, source),
+            ("slope_two", slope_two_in, slope_two),
+            ("slope_low", slope_low_in, slope_low),
+            ("back_two", back_two_in, back_two),
+            ("back_high", back_high_in, back_high),
+        )
+    ):
+        loads[name] = pltpu.make_async_copy(src, dst, load_sems.at[number])
+        loads[name].start()
+
+    def ready(*names):
+        for name in names:
+            loads[name].wait()
 
     def remote(src, dst, number, target):
         return pltpu.make_async_remote_copy(
@@ -199,9 +236,11 @@
     def take(first, second):
         return swap_rows((first[0:5], first[4:9], second[0:5], second[4:9]))
 
+    ready("uf", "ua")
     for comp in range(3):
         for place, value in enumerate(take(uf[comp], ua[comp])):
             u[place, comp] = value
+    ready("lam", "mu")
     lam_here, mu_here = take(lam[...], lam[...]), take(mu[...], mu[...])
     edge_pair = jnp.where(low2, mu_here[0], lam_here[0])
     send_a[...] = pack_half(
@@ -211,10 +250,12 @@
     copy_a = remote(send_a, recv_a, 0, (left, event))
     copy_a.start()
 
+    ready("rho")
     rho_here = take(rho[...], rho[...])
     for place in range(4):
         weight = 0.2 if place == 0 else float(weights[place])
         im[place] = time_step / (rho_here[place] * (weight * (node_weight * lane_weight)))
+    ready("vf", "va", "source")
     for comp in range(3):
         rates = take(vf[comp], va[comp])
         sources = take(jnp.zeros_like(source[comp]), source[comp])
@@ -298,6 +339,7 @@
                 value = f[i, c] + total[i, c] + combine(numbers[:, i], [sx[p, c] for p in range(5)])
                 f[i, c] = middle_sum(value)
 
+    ready("slope_two", "slope_low", "back_two", "back_high")
     slopes(0, 4)
     copy_a.wait_recv()
     arrived = unpack_half(recv_a[...], 20)
@@ -428,11 +470,20 @@
         copy.wait_send()
 
 
+def flush(*refs):
+    copies = [pltpu.make_async_copy(refs[n], refs[5 + n], refs[10].at[n]) for n in range(5)]
+    for copy in copies:
+        copy.start()
+    for copy in copies:
+        copy.wait()
+
+
 def run(regions, events, interpret, *arrays):
     lanes = arrays[0].shape[-1]
     fields = [jnp.transpose(array[0], (0, 2, 1, 3)) for array in arrays[:5]]
     models = [jnp.transpose(array, (1, 0, 2)) for array in arrays[5:]]
     tables = [jnp.asarray(table) for table in lane_tables(lanes)]
+    operands = [*fields, *models, *tables]
     planes = 8 // events
     state = jax.ShapeDtypeStruct((3, 9, 8, lanes), jnp.float32)
     f32 = jnp.float32
@@ -446,7 +497,7 @@
     outs = pl.pallas_call(
         functools.partial(kernel, regions, events),
         out_shape=[state] * 4 + [jax.ShapeDtypeStruct((2, 9, planes, lanes), f32)],
-        in_specs=[pl.BlockSpec(memory_space=pltpu.VMEM)] * 12,
+        in_specs=[pl.BlockSpec(memory_space=pltpu.HBM)] * 12,
         out_specs=[pl.BlockSpec(memory_space=pltpu.VMEM)] * 5,
         scratch_shapes=[
             vector,
@@ -476,12 +527,22 @@
             pltpu.SemaphoreType.DMA((2, 6)),
             pltpu.SemaphoreType.DMA((events,)),
             pltpu.SemaphoreType.DMA((2, max(events - 1, 1))),
+            *[pltpu.VMEM(array.shape, array.dtype) for array in operands],
+            pltpu.SemaphoreType.DMA((len(operands),)),
         ],
         compiler_params=pltpu.CompilerParams(
-            collective_id=0, has_side_effects=True, vmem_limit_bytes=40 * 1024 * 1024
+            collective_id=0, has_side_effects=True, vmem_limit_bytes=63 * 1024 * 1024
         ),
         name="adjoint_steps",
-    )(*fields, *models, *tables)
+    )(*operands)
+    outs = pl.pallas_call(
+        flush,
+        out_shape=[jax.ShapeDtypeStruct(out.shape, out.dtype) for out in outs],
+        in_specs=[pl.BlockSpec(memory_space=pl.ANY)] * 5,
+        out_specs=[pl.BlockSpec(memory_space=pltpu.HBM)] * 5,
+        scratch_shapes=[pltpu.SemaphoreType.DMA((5,))],
+        name="write_out",
+    )(*outs)
     forward, forward_rate, adjoint, adjoint_rate = [
         jnp.transpose(out, (0, 2, 1, 3))[None] for out in outs[:4]
     ]

time: 33.2 us -> 35.9 us (1.081); the launches traced: 32.7 us -> 35.7 us
  Pallas kernels: 18.5 us -> 35.1 us
  local copies, waits for them, and re-layouts: 13.5 us -> 0 us
    pallas_call x0 -> x1, Pallas kernels: none -> 15.7 us  [run(): pl.pallas_call(flush, out_shape=[jax.ShapeDtypeStruct(out.shape, out.dtyp...]
    unnamed x29 -> x0, local copies, waits for them, and re-layouts: 13.5 us -> none
    pallas_call x1, Pallas kernels: 18.5 us -> 19.4 us  [run(): pl.pallas_call(functools.partial(kernel, regions, events), out_shape=[sta...]
where the time goes in v1:
time: 35.9 us; the launch traced here: 35.7 us
  Pallas kernels  35.1 us (98%)
  between operations  0.64 us (2%)
    pallas_call x1, Pallas kernels, run(): pl.pallas_call(functools.partial(kernel, regions, events), out_shape=[sta...  19.4 us
    pallas_call x1, Pallas kernels, run(): pl.pallas_call(flush, out_shape=[jax.ShapeDtypeStruct(out.shape, out.dtyp...  15.7 us

profile of v1, /device:TPU:0, one launch (start us, length us, event | category | flops | bytes accessed | tf_op | source)
XLA Modules:
  0.0 35.7 jit_solution(14533974688935855566)
XLA Ops:
  0.6 19.4 %adjoint_steps.1 = (f32[3,9,8,128]{3,2,1,0:T(8,128)}, f32[3,9,8,128]{3,2,1,0:T(8,128)}, f32[3,9,8,128]{3,2,1,0:T(8,128)}, f32[3,9,8,128]{3,2,1,0:T(8,128)}, f32[2,9,4,128]{3,2,1,0:T(4,128)}) custom-call(f32[3,9,8,128]{3,2,1,0:T(8,128)} %bitcast.31, f32[3,9,8,128]{3,2,1,0:T(8,128)} %bitcast.32, f32[3,9,8,128]{3,2,1,0:T(8,128)} %bitcast.33, ...), custom_call_target="tpu_custom_call" | custom-call | tf_op jit(solution)/shard_map/adjoint_steps/pallas_call | solution.py:497
  20.1 15.7 %write_out.1 = (f32[3,9,8,128]{3,2,1,0:T(8,128)}, f32[3,9,8,128]{3,2,1,0:T(8,128)}, f32[3,9,8,128]{3,2,1,0:T(8,128)}, f32[3,9,8,128]{3,2,1,0:T(8,128)}, f32[2,9,4,128]{3,2,1,0:T(4,128)}) custom-call(f32[3,9,8,128]{3,2,1,0:T(8,128)} %get-tuple-element.15.refs_0_, f32[3,9,8,128]{3,2,1,0:T(8,128)} %get-tuple-element.16.refs_1_, ...), custom_call_target="tpu_custom_call" | custom-call | tf_op jit(solution)/shard_map/write_out/pallas_call | solution.py:538

commit v2 on v1

--- a/solution.py
+++ b/solution.py
@@ -471,11 +471,16 @@
 
 
 def flush(*refs):
-    copies = [pltpu.make_async_copy(refs[n], refs[5 + n], refs[10].at[n]) for n in range(5)]
-    for copy in copies:
-        copy.start()
-    for copy in copies:
-        copy.wait()
+    sources, outs, held, sems = refs[:5], refs[5:10], refs[10:15], refs[15]
+    loads = [pltpu.make_async_copy(sources[n], held[n], sems.at[0, n]) for n in range(5)]
+    stores = [pltpu.make_async_copy(held[n], outs[n], sems.at[1, n]) for n in range(5)]
+    for load in loads:
+        load.start()
+    for load, store in zip(loads, stores):
+        load.wait()
+        store.start()
+    for store in stores:
+        store.wait()
 
 
 def run(regions, events, interpret, *arrays):
@@ -535,12 +540,17 @@
         ),
         name="adjoint_steps",
     )(*operands)
+    shapes = [jax.ShapeDtypeStruct(out.shape, out.dtype) for out in outs]
     outs = pl.pallas_call(
         flush,
-        out_shape=[jax.ShapeDtypeStruct(out.shape, out.dtype) for out in outs],
-        in_specs=[pl.BlockSpec(memory_space=pl.ANY)] * 5,
+        out_shape=shapes,
+        in_specs=[pl.BlockSpec(memory_space=pltpu.HBM)] * 5,
         out_specs=[pl.BlockSpec(memory_space=pltpu.HBM)] * 5,
-        scratch_shapes=[pltpu.SemaphoreType.DMA((5,))],
+        scratch_shapes=[
+            *[pltpu.VMEM(shape.shape, shape.dtype) for shape in shapes],
+            pltpu.SemaphoreType.DMA((2, 5)),
+        ],
+        compiler_params=pltpu.CompilerParams(vmem_limit_bytes=63 * 1024 * 1024),
         name="write_out",
     )(*outs)
     forward, forward_rate, adjoint, adjoint_rate = [

time: 35.9 us -> 22 us (0.61)
  Pallas kernels: 35.1 us -> 21.2 us
    pallas_call x1, Pallas kernels: 15.7 us -> 1.8 us  [run(): pl.pallas_call(flush, out_shape=shapes, in_specs=[pl.BlockSpec(memory_spa...]
where the time goes in v2:
time: 22 us; the launch traced here: 21.9 us
  Pallas kernels  21.2 us (96%)
  between operations  0.64 us (3%)
    pallas_call x1, Pallas kernels, run(): pl.pallas_call(functools.partial(kernel, regions, events), out_shape=[sta...  19.4 us
    pallas_call x1, Pallas kernels, run(): pl.pallas_call(flush, out_shape=shapes, in_specs=[pl.BlockSpec(memory_spa...  1.8 us

profile of v2, /device:TPU:0, one launch (start us, length us, event | category | flops | bytes accessed | tf_op | source)
XLA Modules:
  0.0 21.9 jit_solution(5557898832445488682)
XLA Ops:
  0.6 19.4 %adjoint_steps.1 = (f32[3,9,8,128]{3,2,1,0:T(8,128)}, f32[3,9,8,128]{3,2,1,0:T(8,128)}, f32[3,9,8,128]{3,2,1,0:T(8,128)}, f32[3,9,8,128]{3,2,1,0:T(8,128)}, f32[2,9,4,128]{3,2,1,0:T(4,128)}) custom-call(f32[3,9,8,128]{3,2,1,0:T(8,128)} %bitcast.31, f32[3,9,8,128]{3,2,1,0:T(8,128)} %bitcast.32, f32[3,9,8,128]{3,2,1,0:T(8,128)} %bitcast.33, ...), custom_call_target="tpu_custom_call" | custom-call | tf_op jit(solution)/shard_map/adjoint_steps/pallas_call | solution.py:502
  20.1 1.8 %write_out.1 = (f32[3,9,8,128]{3,2,1,0:T(8,128)}, f32[3,9,8,128]{3,2,1,0:T(8,128)}, f32[3,9,8,128]{3,2,1,0:T(8,128)}, f32[3,9,8,128]{3,2,1,0:T(8,128)}, f32[2,9,4,128]{3,2,1,0:T(4,128)}) custom-call(f32[3,9,8,128]{3,2,1,0:T(8,128)} %get-tuple-element.15.refs_0_, f32[3,9,8,128]{3,2,1,0:T(8,128)} %get-tuple-element.16.refs_1_, ...), custom_call_target="tpu_custom_call" | custom-call | tf_op jit(solution)/shard_map/write_out/pallas_call | solution.py:544

commit v3 on v1

--- a/solution.py
+++ b/solution.py
@@ -325,18 +325,17 @@
             both_kinds = jnp.where(low2, k1, turn(k2, 2))
             kacc[i] = both_kinds if step == 0 else kacc[i] + both_kinds
 
-    def gather_forces():
-        rows = 600
-        values = sy[...].reshape(rows, 2 * lanes)
-        high = values.astype(jnp.bfloat16)
-        low = (values - high.astype(jnp.float32)).astype(jnp.bfloat16)
-        first = jnp.dot(high, back_two[...], preferred_element_type=jnp.float32)
-        total = first[:, :lanes] + first[:, lanes:]
-        total = total + jnp.dot(low, back_high[...], preferred_element_type=jnp.float32)
-        total = total.reshape(5, 3, 5, 8, lanes)
-        for i in (0, 4, 1, 2, 3):
+    def gather_forces(*places):
+        for i in places:
+            values = sy[i].reshape(120, 2 * lanes)
+            high = values.astype(jnp.bfloat16)
+            low = (values - high.astype(jnp.float32)).astype(jnp.bfloat16)
+            first = jnp.dot(high, back_two[...], preferred_element_type=jnp.float32)
+            total = first[:, :lanes] + first[:, lanes:]
+            total = total + jnp.dot(low, back_high[...], preferred_element_type=jnp.float32)
+            total = total.reshape(3, 5, 8, lanes)
             for c in range(3):
-                value = f[i, c] + total[i, c] + combine(numbers[:, i], [sx[p, c] for p in range(5)])
+                value = f[i, c] + total[c] + combine(numbers[:, i], [sx[p, c] for p in range(5)])
                 f[i, c] = middle_sum(value)
 
     ready("slope_two", "slope_low", "back_two", "back_high")
@@ -353,13 +352,15 @@
     lamw[4] = turn(jnp.where(low4, lam_next, lam_here[0]), 4) * weight
     slopes(4, 5)
     strains(0)
-    gather_forces()
+    gather_forces(4)
+    send_r[0] = pack_half(f[4].reshape(15, 8, lanes), False)
+    copy_r = remote(send_r.at[0], recv_r.at[0], 3, (right, event))
+    copy_r.start()
+    gather_forces(0)
     send_l[...] = pack_half(f[0].reshape(15, 8, lanes), True)
-    send_r[0] = pack_half(f[4].reshape(15, 8, lanes), False)
     copy_l = remote(send_l, recv_l, 2, (left, event))
     copy_l.start()
-    copy_r = remote(send_r.at[0], recv_r.at[0], 3, (right, event))
-    copy_r.start()
+    gather_forces(1, 2, 3)
 
     def advance(place, force):
         for c in range(3):
@@ -396,7 +397,7 @@
     slopes(0, 1)
     slopes(4, 5)
     strains(1)
-    gather_forces()
+    gather_forces(4)
     send_r[1] = pack_half(f[4].reshape(15, 8, lanes), False)
     copy_s = remote(send_r.at[1], recv_r.at[1], 4, (right, event))
     copy_s.start()
@@ -433,6 +434,7 @@
         copy.start()
         copies.append(copy)
 
+    gather_forces(0, 1, 2, 3)
     for place in (1, 2, 3):
         advance(place, f[place])
     copy_s.wait_recv()
@@ -471,11 +473,12 @@
 
 
 def flush(*refs):
-    copies = [pltpu.make_async_copy(refs[n], refs[5 + n], refs[10].at[n]) for n in range(5)]
-    for copy in copies:
-        copy.start()
-    for copy in copies:
-        copy.wait()
+    sources, outs, sems = refs[:5], refs[5:10], refs[10]
+    stores = [pltpu.make_async_copy(sources[n], outs[n], sems.at[n]) for n in range(5)]
+    for store in stores:
+        store.start()
+    for store in stores:
+        store.wait()
 
 
 def run(regions, events, interpret, *arrays):
@@ -484,6 +487,7 @@
     models = [jnp.transpose(array, (1, 0, 2)) for array in arrays[5:]]
     tables = [jnp.asarray(table) for table in lane_tables(lanes)]
     operands = [*fields, *models, *tables]
+    operands = [pltpu.with_memory_space_constraint(array, pltpu.HBM) for array in operands]
     planes = 8 // events
     state = jax.ShapeDtypeStruct((3, 9, 8, lanes), jnp.float32)
     f32 = jnp.float32
@@ -531,16 +535,19 @@
             pltpu.SemaphoreType.DMA((len(operands),)),
         ],
         compiler_params=pltpu.CompilerParams(
-            collective_id=0, has_side_effects=True, vmem_limit_bytes=63 * 1024 * 1024
+            collective_id=0, has_side_effects=True, vmem_limit_bytes=40 * 1024 * 1024
         ),
         name="adjoint_steps",
     )(*operands)
+    shapes = [jax.ShapeDtypeStruct(out.shape, out.dtype) for out in outs]
+    shapes = [jax.ShapeDtypeStruct(out.shape, out.dtype) for out in outs]
     outs = pl.pallas_call(
         flush,
-        out_shape=[jax.ShapeDtypeStruct(out.shape, out.dtype) for out in outs],
-        in_specs=[pl.BlockSpec(memory_space=pl.ANY)] * 5,
+        out_shape=shapes,
+        in_specs=[pl.BlockSpec(memory_space=pltpu.VMEM)] * 5,
         out_specs=[pl.BlockSpec(memory_space=pltpu.HBM)] * 5,
         scratch_shapes=[pltpu.SemaphoreType.DMA((5,))],
+        compiler_params=pltpu.CompilerParams(vmem_limit_bytes=16 * 1024 * 1024),
         name="write_out",
     )(*outs)
     forward, forward_rate, adjoint, adjoint_rate = [

time: 35.9 us -> 19.7 us (0.55)
  Pallas kernels: 35.1 us -> 19 us
    pallas_call x1, Pallas kernels: 15.7 us -> 0.81 us  [run(): pl.pallas_call(flush, out_shape=shapes, in_specs=[pl.BlockSpec(memory_spa...]
    pallas_call x1, Pallas kernels: 19.4 us -> 18.1 us  [run(): pl.pallas_call(functools.partial(kernel, regions, events), out_shape=[sta...]
where the time goes in v3:
time: 19.7 us; the launch traced here: 19.6 us
  Pallas kernels  19 us (96%)
  between operations  0.64 us (3%)
    pallas_call x1, Pallas kernels, run(): pl.pallas_call(functools.partial(kernel, regions, events), out_shape=[sta...  18.1 us
    pallas_call x1, Pallas kernels, run(): pl.pallas_call(flush, out_shape=shapes, in_specs=[pl.BlockSpec(memory_spa...  0.81 us

profile of v3, /device:TPU:0, one launch (start us, length us, event | category | flops | bytes accessed | tf_op | source)
XLA Modules:
  0.0 19.6 jit_solution(13748124016554220605)
XLA Ops:
  0.6 18.1 %adjoint_steps.1 = (f32[3,9,8,128]{3,2,1,0:T(8,128)S(1)}, f32[3,9,8,128]{3,2,1,0:T(8,128)S(1)}, f32[3,9,8,128]{3,2,1,0:T(8,128)S(1)}, f32[3,9,8,128]{3,2,1,0:T(8,128)S(1)}, f32[2,9,4,128]{3,2,1,0:T(4,128)S(1)}) custom-call(f32[3,9,8,128]{3,2,1,0:T(8,128)} %bitcast.31, f32[3,9,8,128]{3,2,1,0:T(8,128)} %bitcast.32, f32[3,9,8,128]{3,2,1,0:T(8,128)} %bitcast.33, ...), custom_call_target="tpu_custom_call" | custom-call | tf_op jit(solution)/shard_map/adjoint_steps/pallas_call | solution.py:501
  18.8 0.8 %write_out.1 = (f32[3,9,8,128]{3,2,1,0:T(8,128)}, f32[3,9,8,128]{3,2,1,0:T(8,128)}, f32[3,9,8,128]{3,2,1,0:T(8,128)}, f32[3,9,8,128]{3,2,1,0:T(8,128)}, f32[2,9,4,128]{3,2,1,0:T(4,128)}) custom-call(f32[3,9,8,128]{3,2,1,0:T(8,128)S(1)} %get-tuple-element.15.refs_0_, f32[3,9,8,128]{3,2,1,0:T(8,128)S(1)} %get-tuple-element.16.refs_1_, ...), custom_call_target="tpu_custom_call" | custom-call | tf_op jit(solution)/shard_map/write_out/pallas_call | solution.py:544

commit v4 on v3

--- a/solution.py
+++ b/solution.py
@@ -285,7 +285,7 @@
         ) + jnp.dot(high, slope_low[...], preferred_element_type=jnp.float32)
         gy[begin:end] = found.reshape(end - begin, 3, 5, 8, 2 * lanes)
 
-    def strains(step):
+    def strains(step, forces=True, kinds=True):
         for i in range(5):
             gx = [combine(numbers[i], [u[q, c] for q in range(5)]) for c in range(3)]
             gz = []
@@ -297,21 +297,24 @@
             m, l = muw[i], lamw[i]
             xz, xy, zy = gx[1] + gz[0], gx[2] + gm[0], gz[2] + gm[1]
             dilation = gx[0] + gz[1] + gm[2]
-            both = m + m
-            press = l * dilation
-            s_xz, s_xy, s_zy = m * xz, m * xy, m * zy
-            sx[i, 0] = both * gx[0] + press
-            sx[i, 1] = s_xz
-            sx[i, 2] = s_xy
-            sy[i, 0, :, :, :lanes] = s_xy
-            sy[i, 1, :, :, :lanes] = s_zy
-            sy[i, 2, :, :, :lanes] = both * gm[2] + press
-            sy[i, 0, :, :, lanes:] = m * gd[0]
-            sy[i, 1, :, :, lanes:] = m * gd[1]
-            sy[i, 2, :, :, lanes:] = (both + l) * gd[2]
-            for c, stress in enumerate((s_xz, both * gz[1] + press, s_zy)):
-                levels = [stress[q] for q in range(5)]
-                f[i, c] = jnp.stack([combine(numbers[:, k], levels) for k in range(5)])
+            if forces:
+                both = m + m
+                press = l * dilation
+                s_xz, s_xy, s_zy = m * xz, m * xy, m * zy
+                sx[i, 0] = both * gx[0] + press
+                sx[i, 1] = s_xz
+                sx[i, 2] = s_xy
+                sy[i, 0, :, :, :lanes] = s_xy
+                sy[i, 1, :, :, :lanes] = s_zy
+                sy[i, 2, :, :, :lanes] = both * gm[2] + press
+                sy[i, 0, :, :, lanes:] = m * gd[0]
+                sy[i, 1, :, :, lanes:] = m * gd[1]
+                sy[i, 2, :, :, lanes:] = (both + l) * gd[2]
+                for c, stress in enumerate((s_xz, both * gz[1] + press, s_zy)):
+                    levels = [stress[q] for q in range(5)]
+                    f[i, c] = jnp.stack([combine(numbers[:, k], levels) for k in range(5)])
+            if not kinds:
+                continue
 
             def product(value):
                 return value * turn(value, -2)
@@ -351,7 +354,7 @@
     muw[4] = turn(jnp.where(low4, mu_next, mu_here[0]), 4) * weight
     lamw[4] = turn(jnp.where(low4, lam_next, lam_here[0]), 4) * weight
     slopes(4, 5)
-    strains(0)
+    strains(0, kinds=False)
     gather_forces(4)
     send_r[0] = pack_half(f[4].reshape(15, 8, lanes), False)
     copy_r = remote(send_r.at[0], recv_r.at[0], 3, (right, event))
@@ -360,6 +363,7 @@
     send_l[...] = pack_half(f[0].reshape(15, 8, lanes), True)
     copy_l = remote(send_l, recv_l, 2, (left, event))
     copy_l.start()
+    strains(0, forces=False)
     gather_forces(1, 2, 3)
 
     def advance(place, force):

time: 19.7 us -> 19.7 us (level)
  no operation moved by 1% of the time
where the time goes in v4:
time: 19.7 us; the launch traced here: 19.6 us
  Pallas kernels  19 us (96%)
  between operations  0.64 us (3%)
    pallas_call x1, Pallas kernels, run(): pl.pallas_call(functools.partial(kernel, regions, events), out_shape=[sta...  18.1 us
    pallas_call x1, Pallas kernels, run(): pl.pallas_call(flush, out_shape=shapes, in_specs=[pl.BlockSpec(memory_spa...  0.81 us

profile of v4, /device:TPU:0, one launch (start us, length us, event | category | flops | bytes accessed | tf_op | source)
XLA Modules:
  0.0 19.6 jit_solution(4321180450180440935)
XLA Ops:
  0.6 18.1 %adjoint_steps.1 = (f32[3,9,8,128]{3,2,1,0:T(8,128)S(1)}, f32[3,9,8,128]{3,2,1,0:T(8,128)S(1)}, f32[3,9,8,128]{3,2,1,0:T(8,128)S(1)}, f32[3,9,8,128]{3,2,1,0:T(8,128)S(1)}, f32[2,9,4,128]{3,2,1,0:T(4,128)S(1)}) custom-call(f32[3,9,8,128]{3,2,1,0:T(8,128)} %bitcast.31, f32[3,9,8,128]{3,2,1,0:T(8,128)} %bitcast.32, f32[3,9,8,128]{3,2,1,0:T(8,128)} %bitcast.33, ...), custom_call_target="tpu_custom_call" | custom-call | tf_op jit(solution)/shard_map/adjoint_steps/pallas_call | solution.py:505
  18.8 0.8 %write_out.1 = (f32[3,9,8,128]{3,2,1,0:T(8,128)}, f32[3,9,8,128]{3,2,1,0:T(8,128)}, f32[3,9,8,128]{3,2,1,0:T(8,128)}, f32[3,9,8,128]{3,2,1,0:T(8,128)}, f32[2,9,4,128]{3,2,1,0:T(4,128)}) custom-call(f32[3,9,8,128]{3,2,1,0:T(8,128)S(1)} %get-tuple-element.15.refs_0_, f32[3,9,8,128]{3,2,1,0:T(8,128)S(1)} %get-tuple-element.16.refs_1_, ...), custom_call_target="tpu_custom_call" | custom-call | tf_op jit(solution)/shard_map/write_out/pallas_call | solution.py:548
